TPU v7x, 32 devices: a whole 2x2x4 slice. The times are simulated.
32 devices in a mesh: seq: 8 (over y, x, core), ch: 4 (over z).
Axes of the slice: x: 2, y: 2, z: 4, core: 2. Of those that a mesh axis runs over, the one named last changes fastest.
Arguments:
- dna_features: bfloat16 [2, 512, 1280], P(None, 'seq'), may hold values from -6 to 6
- gain_a: float32 [1280], replicated, may hold values from 0.25 to 1.75
- conv_a: bfloat16 [5, 1280, 1408], P(None, 'seq', 'ch'), may hold values from -0.078125 to 0.078125
- bias_a: float32 [1408], P('ch'), may hold values from -3 to 3
- gain_b: float32 [1408], replicated, may hold values from 0.25 to 1.75
- conv_b: bfloat16 [5, 1408, 1536], P(None, 'seq', 'ch'), may hold values from -0.0625 to 0.0625
- bias_b: float32 [1536], P('ch'), may hold values from -3 to 3
- grad_out: bfloat16 [2, 128, 1536], P(None, 'seq', 'ch'), may hold values from -6 to 6
Outputs:
- pooled_out: bfloat16 [2, 128, 1536], P(None, 'seq', 'ch')
- input_grad: bfloat16 [2, 512, 1280], P(None, 'seq', 'ch')
All inputs are finite; a program needn't handle non-finite values.
Results may differ from a plain program's by a relative error of at most 0.018.
Values may be sent and summed in bfloat16 or wider, within the bound.
No kernel may reach another device: no remote copies, remote signals or barrier semaphores. Data moves between devices by JAX's collectives and lax.ppermute only.
A program may use at most 128 MiB of HBM per device.

v0:
```python
import math
import jax
import jax.numpy as jnp
from jax import lax
from jax.sharding import PartitionSpec as P

EPS = 1e-06
ROOT = math.sqrt(2.0 / math.pi)


def with_halo(block, sides, width):
    for axis, dim in sides:
        count = lax.axis_size(axis)
        forward = [(i, i + 1) for i in range(count - 1)]
        backward = [(target, source) for source, target in forward]
        low = lax.ppermute(
            lax.slice_in_dim(block, block.shape[dim] - width, None, axis=dim), axis, forward
        )
        high = lax.ppermute(lax.slice_in_dim(block, 0, width, axis=dim), axis, backward)
        block = jnp.concatenate([low, block, high], axis=dim)
    return block


def gelu_tanh(z):
    return 0.5 * z * (1.0 + jnp.tanh(ROOT * (z + 0.044715 * z * z * z)))


def gelu_slope(z):
    t = jnp.tanh(ROOT * (z + 0.044715 * z * z * z))
    return 0.5 * (1.0 + t) + 0.5 * z * (1.0 - t * t) * ROOT * (1.0 + 3.0 * 0.044715 * z * z)


def pool_pairs(v):
    return v.reshape(v.shape[0], v.shape[1] // 2, 2, v.shape[2]).sum(axis=2) * 0.5


def repeat_half(v):
    return (jnp.repeat(v.astype(jnp.float32), 2, axis=1) * 0.5).astype(jnp.bfloat16)


def conv_rows(padded, weight, length):
    total = jnp.einsum(
        "wtc,co->wto", padded[:, 0:length], weight[0], preferred_element_type=jnp.float32
    )
    for offset in range(1, weight.shape[0]):
        total = total + jnp.einsum(
            "wtc,co->wto",
            padded[:, offset : offset + length],
            weight[offset],
            preferred_element_type=jnp.float32,
        )
    return total


def conv_back(padded, weight, length):
    total = jnp.einsum(
        "wto,co->wtc", padded[:, 4 : 4 + length], weight[0], preferred_element_type=jnp.float32
    )
    for offset in range(1, weight.shape[0]):
        start = 4 - offset
        total = total + jnp.einsum(
            "wto,co->wtc",
            padded[:, start : start + length],
            weight[offset],
            preferred_element_type=jnp.float32,
        )
    return total


def per_device(dna_features, gain_a, conv_a, bias_a, gain_b, conv_b, bias_b, grad_out):
    rows_in = dna_features.shape[1]
    rows_mid = rows_in // 2
    width_in = dna_features.shape[2]
    width_mid = gain_b.shape[0]
    share_mid = bias_a.shape[0]
    share_in = width_in // lax.axis_size("ch")
    ch_index = lax.axis_index("ch")
    whole_a, whole_b = (
        lax.all_gather(conv_a, "seq", axis=1, tiled=True),
        lax.all_gather(conv_b, "seq", axis=1, tiled=True),
    )
    feat = dna_features.astype(jnp.float32)
    scale_a = lax.rsqrt(jnp.mean(feat * feat, axis=-1, keepdims=True) + EPS)
    act_a = gelu_tanh(feat * scale_a * gain_a).astype(jnp.bfloat16)
    padded_a = with_halo(act_a, (("seq", 1),), 2)
    conv_out_a = conv_rows(padded_a, whole_a, rows_in)
    mid = pool_pairs(conv_out_a + bias_a).astype(jnp.bfloat16)
    gain_part = lax.dynamic_slice_in_dim(gain_b, ch_index * share_mid, share_mid, 0)
    mid_f = mid.astype(jnp.float32)
    squares = lax.psum(jnp.sum(mid_f * mid_f, axis=-1, keepdims=True), "ch")
    scale_b = lax.rsqrt(squares / width_mid + EPS)
    act_part = gelu_tanh(mid_f * scale_b * gain_part).astype(jnp.bfloat16)
    act_full = lax.all_gather(act_part, "ch", axis=2, tiled=True)
    padded_b = with_halo(act_full, (("seq", 1),), 2)
    conv_out_b = conv_rows(padded_b, whole_b, rows_mid)
    pooled_out = pool_pairs(conv_out_b + bias_b).astype(jnp.bfloat16)
    grad_b = repeat_half(grad_out)
    grad_pad_b = with_halo(grad_b, (("seq", 1),), 2)
    partial_b = conv_back(grad_pad_b, whole_b, rows_mid)
    back_share = lax.psum_scatter(
        partial_b.astype(jnp.bfloat16), "ch", scatter_dimension=2, tiled=True
    ).astype(jnp.float32)
    normed_b = mid_f * scale_b
    grad_n = back_share * gelu_slope(normed_b * gain_part) * gain_part
    inner_b = lax.psum(jnp.sum(grad_n * normed_b, axis=-1, keepdims=True), "ch") / width_mid
    grad_mid = (scale_b * (grad_n - normed_b * inner_b)).astype(jnp.bfloat16)
    grad_a = repeat_half(grad_mid)
    grad_pad_a = with_halo(grad_a, (("seq", 1),), 2)
    partial_a = conv_back(grad_pad_a, whole_a, rows_in)
    back_share_a = lax.psum_scatter(
        partial_a.astype(jnp.bfloat16), "ch", scatter_dimension=2, tiled=True
    ).astype(jnp.float32)
    feat_part = lax.dynamic_slice_in_dim(feat, ch_index * share_in, share_in, 2)
    gain_part_a = lax.dynamic_slice_in_dim(gain_a, ch_index * share_in, share_in, 0)
    normed_a = feat_part * scale_a
    grad_na = back_share_a * gelu_slope(normed_a * gain_part_a) * gain_part_a
    inner_a = lax.psum(jnp.sum(grad_na * normed_a, axis=-1, keepdims=True), "ch") / width_in
    input_grad = (scale_a * (grad_na - normed_a * inner_a)).astype(jnp.bfloat16)
    return (pooled_out, input_grad)


def solution(mesh):
    in_specs = (
        P(None, "seq", None),
        P(),
        P(None, "seq", "ch"),
        P("ch"),
        P(),
        P(None, "seq", "ch"),
        P("ch"),
        P(None, "seq", "ch"),
    )
    out_specs = (P(None, "seq", "ch"), P(None, "seq", "ch"))
    return jax.shard_map(
        per_device, mesh=mesh, in_specs=in_specs, out_specs=out_specs, check_vma=False
    )
```

profile of v0, /device:TPU:0, one launch (start us, length us, event | category | flops | bytes accessed | tf_op | source)
XLA Modules:
  0.0 215.0 jit_solution(2797888684650728712)
XLA Ops:
  7.2 0.7 all-gather.3.cloned.1.call-update
  7.9 0.7 all-gather.5.cloned.1.call-update
  8.7 1.1 multiply_reduce_fusion
  9.8 1.3 fusion.28
  11.2 1.3 collective-permute-start.1
  12.5 3.0 %collective-permute-start = (bf16[2,2,1280]{2,1,0:T(2,128)(2,1)S(1)}, bf16[2,2,1280]{2,1,0:T(2,128)(2,1)S(1)}, u32[]{:S(2)}, u32[]{:S(2)}) collective-permute-start(bf16[2,2,1280]{2,1,0:T(2,128)(2,1)S(1)} %get-tuple-element.4), channel_id=1, source_target_pairs={{0,4},{4,8},{8,12},{12,16},{16,20},{20,24},{24,28},{1,5},{5,9},{9,... | collective-permute-start | bytes 30728 | tf_op jit(solution)/shard_map/ppermute | solution.py:16
  15.5 0.7 multiply_convert_fusion.3
  16.4 4.5 %collective-permute-start.5 = (bf16[2,2,384]{2,1,0:T(2,128)(2,1)S(1)}, bf16[2,2,384]{2,1,0:T(2,128)(2,1)S(1)}, u32[]{:S(2)}, u32[]{:S(2)}) collective-permute-start(bf16[2,2,384]{2,1,0:T(2,128)(2,1)S(1)} %get-tuple-element.13), channel_id=1, source_target_pairs={{0,4},{4,8},{8,12},{12,16},{16,20},{20,24},{24,28},{1,5},{5,9},{9,... | collective-permute-start | bytes 9224 | tf_op jit(solution)/shard_map/ppermute | solution.py:16
  20.9 1.3 collective-permute-start.4
  22.2 1.0 convert_element_type.60
  23.2 0.8 dynamic_slice.11
  24.0 0.8 dynamic_slice.9
  24.8 27.5 %all-gather.3.cloned.1.call-done = bf16[5,1280,352]{2,1,0:T(8,128)(2,1)} async-done(((bf16[5,160,352]{2,1,0:T(8,128)(2,1)}), bf16[5,1280,352]{2,1,0:T(8,128)(2,1)}) %all-gather.3.cloned.1.call-update) | async-done | bytes 4505616 | tf_op jit(solution)/shard_map/all_gather | solution.py:79
  52.3 1.5 fusion.23
  53.8 1.5 fusion.19
  55.4 1.5 fusion.21
  56.9 1.5 fusion.8
  58.5 1.5 fusion.7
  60.0 0.1 reshape.33
  60.1 0.2 reduce_sum.55
  60.4 35.6 %all-gather.5.cloned.1.call-done = bf16[5,1408,384]{2,1,0:T(8,128)(2,1)} async-done(((bf16[5,176,384]{2,1,0:T(8,128)(2,1)}), bf16[5,1408,384]{2,1,0:T(8,128)(2,1)}) %all-gather.5.cloned.1.call-update) | async-done | bytes 5406736 | tf_op jit(solution)/shard_map/all_gather | solution.py:80
  95.9 1.7 fusion.14
  97.6 1.7 fusion.16
  99.3 1.7 fusion.12
  101.0 1.7 fusion.4
  102.7 1.7 fusion.5
  104.4 1.0 copy.34
  105.5 1.1 reshape.45
  106.6 0.1 fusion.66
  106.7 11.8 %psum.21 = f32[2,32,1]{1,0,2:T(2,128)S(1)} all-reduce(f32[2,32,1]{1,0,2:T(2,128)S(1)} %bitcast.81), channel_id=1, replica_groups=mesh['seq'=8,'ch'=4] {'ch'}, use_global_device_ids=true, to_apply=%region_3.0 | all-reduce | flops 64 | bytes 512 | tf_op jit(solution)/shard_map/psum | solution.py:90
  118.5 8.7 %reduce-scatter.7.cloned.1.call-done = bf16[352,64]{1,0:T(8,128)(2,1)} async-done(((bf16[1408,64]{1,0:T(8,128)(2,1)}), bf16[352,64]{1,0:T(8,128)(2,1)}) %reduce-scatter.7.cloned.1.call-update) | async-done | bytes 45072
  127.3 1.0 reshape.46
  128.3 0.1 copy.35
  128.4 0.2 fusion.62
  128.6 8.8 %psum.22 = f32[2,32,1]{1,0,2:T(2,128)S(1)} all-reduce(f32[2,32,1]{1,0,2:T(2,128)S(1)} %bitcast.82), channel_id=1, replica_groups=mesh['seq'=8,'ch'=4] {'ch'}, use_global_device_ids=true, to_apply=%region_7.0 | all-reduce | flops 64 | bytes 512 | tf_op jit(solution)/shard_map/psum | solution.py:105
  137.5 0.2 multiply_convert_fusion.1
  137.7 0.2 copy.28
  137.8 16.1 %all_gather.10 = bf16[2,32,1408]{1,0,2:T(2,128)(2,1)S(1)} all-gather(bf16[2,32,352]{1,0,2:T(2,128)(2,1)S(1)} %copy.28), channel_id=1, replica_groups=mesh['seq'=8,'ch'=4] {'ch'}, dimensions={2}, use_global_device_ids=true | all-gather | bytes 225280 | tf_op jit(solution)/shard_map/all_gather | solution.py:93
  154.0 0.9 copy.29
  154.9 1.3 collective-permute-start.3
  156.2 3.0 %collective-permute-start.2 = (bf16[2,2,1408]{2,1,0:T(2,128)(2,1)S(1)}, bf16[2,2,1408]{2,1,0:T(2,128)(2,1)S(1)}, u32[]{:S(2)}, u32[]{:S(2)}) collective-permute-start(bf16[2,2,1408]{2,1,0:T(2,128)(2,1)S(1)} %get-tuple-element.6), channel_id=1, source_target_pairs={{0,4},{4,8},{8,12},{12,16},{16,20},{20,24},{24,28},{1,5},{5,9},{9,... | collective-permute-start | bytes 33800 | tf_op jit(solution)/shard_map/ppermute | solution.py:16
  159.3 0.1 convert_element_type.74
  159.4 3.1 %collective-permute-start.7 = (bf16[2,2,352]{2,1,0:T(2,128)(2,1)S(1)}, bf16[2,2,352]{2,1,0:T(2,128)(2,1)S(1)}, u32[]{:S(2)}, u32[]{:S(2)}) collective-permute-start(bf16[2,2,352]{2,1,0:T(2,128)(2,1)S(1)} %get-tuple-element.9), channel_id=1, source_target_pairs={{0,4},{4,8},{8,12},{12,16},{16,20},{20,24},{24,28},{1,5},{5,9},{9,... | collective-permute-start | bytes 8456 | tf_op jit(solution)/shard_map/ppermute | solution.py:16
  162.5 1.3 collective-permute-start.6
  163.8 1.5 fusion.15
  165.4 1.6 fusion.20
  167.0 1.6 fusion.22
  168.7 1.6 fusion.18
  170.3 1.6 fusion.1
  171.9 1.6 fusion.2
  173.6 0.5 copy.36
  174.1 1.0 reshape.47
  175.2 1.5 fusion.13
  176.7 1.5 fusion.11
  178.3 1.5 fusion.17
  179.8 1.5 fusion.10
  181.4 0.1 reduce_sum.57
  181.5 0.6 multiply_convert_fusion.4
  182.1 15.3 %reduce-scatter.9.cloned.1.call-done = bf16[320,128]{1,0:T(8,128)(2,1)} async-done(((bf16[1280,128]{1,0:T(8,128)(2,1)}), bf16[320,128]{1,0:T(8,128)(2,1)}) %reduce-scatter.9.cloned.1.call-update) | async-done | bytes 81936
  197.4 1.0 reshape.48
  198.4 0.1 copy.37
  198.6 0.3 multiply_reduce_fusion.1
  198.9 8.6 %psum.23 = f32[2,64,1]{1,0,2:T(2,128)S(1)} all-reduce(f32[2,64,1]{1,0,2:T(2,128)S(1)} %bitcast.83), channel_id=1, replica_groups=mesh['seq'=8,'ch'=4] {'ch'}, use_global_device_ids=true, to_apply=%region_10.0 | all-reduce | flops 128 | bytes 1024 | tf_op jit(solution)/shard_map/psum | solution.py:117
  207.6 0.9 multiply_convert_fusion
  (34 shorter events, 0.5 us)
Async XLA Ops:
  7.2 45.1 %all-gather.3.cloned.1.call-start = ((), (), s32[]{:S(2)}) async-start(), calls=%async_computation.2 | async-start | bytes 5529600 | tf_op jit(solution)/shard_map/all_gather | solution.py:79
  7.9 88.0 %all-gather.5.cloned.1.call-start = ((), (), s32[]{:S(2)}) async-start(), calls=%async_computation.3 | async-start | bytes 6082560 | tf_op jit(solution)/shard_map/all_gather | solution.py:80
  8.6 118.6 %reduce-scatter.7.cloned.1.call-start = ((), (), s32[]{:S(2)}) async-start(), calls=%async_computation.4 | async-start | bytes 450560
  9.8 48.6 %copy-start = (f32[352]{0:T(512)S(1)}, f32[352]{0:T(512)}, u32[]{:S(2)}) copy-start(f32[352]{0:T(512)} %param.11) | copy-start | bytes 4228
  11.2 13.6 %collective-permute-start.1 = (bf16[2,2,1280]{2,1,0:T(2,128)(2,1)S(1)}, bf16[2,2,1280]{2,1,0:T(2,128)(2,1)S(1)}, u32[]{:S(2)}, u32[]{:S(2)}) collective-permute-start(bf16[2,2,1280]{2,1,0:T(2,128)(2,1)S(1)} %get-tuple-element.5), channel_id=1, source_target_pairs={{4,0},{8,4},{12,8},{16,12},{20,16},{24,20},{28,24},{5,1},{9,5},{13... | collective-permute-start | bytes 30728 | tf_op jit(solution)/shard_map/ppermute | solution.py:19
  12.5 41.3 %collective-permute-start = (bf16[2,2,1280]{2,1,0:T(2,128)(2,1)S(1)}, bf16[2,2,1280]{2,1,0:T(2,128)(2,1)S(1)}, u32[]{:S(2)}, u32[]{:S(2)}) collective-permute-start(bf16[2,2,1280]{2,1,0:T(2,128)(2,1)S(1)} %get-tuple-element.4), channel_id=1, source_target_pairs={{0,4},{4,8},{8,12},{12,16},{16,20},{20,24},{24,28},{1,5},{5,9},{9,... | collective-permute-start | bytes 30728 | tf_op jit(solution)/shard_map/ppermute | solution.py:16
  16.4 81.3 %collective-permute-start.5 = (bf16[2,2,384]{2,1,0:T(2,128)(2,1)S(1)}, bf16[2,2,384]{2,1,0:T(2,128)(2,1)S(1)}, u32[]{:S(2)}, u32[]{:S(2)}) collective-permute-start(bf16[2,2,384]{2,1,0:T(2,128)(2,1)S(1)} %get-tuple-element.13), channel_id=1, source_target_pairs={{0,4},{4,8},{8,12},{12,16},{16,20},{20,24},{24,28},{1,5},{5,9},{9,... | collective-permute-start | bytes 9224 | tf_op jit(solution)/shard_map/ppermute | solution.py:16
  20.9 3.9 %collective-permute-start.4 = (bf16[2,2,384]{2,1,0:T(2,128)(2,1)S(1)}, bf16[2,2,384]{2,1,0:T(2,128)(2,1)S(1)}, u32[]{:S(2)}, u32[]{:S(2)}) collective-permute-start(bf16[2,2,384]{2,1,0:T(2,128)(2,1)S(1)} %get-tuple-element.12), channel_id=1, source_target_pairs={{4,0},{8,4},{12,8},{16,12},{20,16},{24,20},{28,24},{5,1},{9,5},{13... | collective-permute-start | bytes 9224 | tf_op jit(solution)/shard_map/ppermute | solution.py:19
  106.6 90.9 %reduce-scatter.9.cloned.1.call-start = ((), (), s32[]{:S(2)}) async-start(), calls=%async_computation.5 | async-start | bytes 409600
  154.9 23.4 %collective-permute-start.3 = (bf16[2,2,1408]{2,1,0:T(2,128)(2,1)S(1)}, bf16[2,2,1408]{2,1,0:T(2,128)(2,1)S(1)}, u32[]{:S(2)}, u32[]{:S(2)}) collective-permute-start(bf16[2,2,1408]{2,1,0:T(2,128)(2,1)S(1)} %get-tuple-element.7), channel_id=1, source_target_pairs={{4,0},{8,4},{12,8},{16,12},{20,16},{24,20},{28,24},{5,1},{9,5},{13... | collective-permute-start | bytes 33800 | tf_op jit(solution)/shard_map/ppermute | solution.py:19
  156.2 19.0 %collective-permute-start.2 = (bf16[2,2,1408]{2,1,0:T(2,128)(2,1)S(1)}, bf16[2,2,1408]{2,1,0:T(2,128)(2,1)S(1)}, u32[]{:S(2)}, u32[]{:S(2)}) collective-permute-start(bf16[2,2,1408]{2,1,0:T(2,128)(2,1)S(1)} %get-tuple-element.6), channel_id=1, source_target_pairs={{0,4},{4,8},{8,12},{12,16},{16,20},{20,24},{24,28},{1,5},{5,9},{9,... | collective-permute-start | bytes 33800 | tf_op jit(solution)/shard_map/ppermute | solution.py:16
  159.4 7.6 %collective-permute-start.7 = (bf16[2,2,352]{2,1,0:T(2,128)(2,1)S(1)}, bf16[2,2,352]{2,1,0:T(2,128)(2,1)S(1)}, u32[]{:S(2)}, u32[]{:S(2)}) collective-permute-start(bf16[2,2,352]{2,1,0:T(2,128)(2,1)S(1)} %get-tuple-element.9), channel_id=1, source_target_pairs={{0,4},{4,8},{8,12},{12,16},{16,20},{20,24},{24,28},{1,5},{5,9},{9,... | collective-permute-start | bytes 8456 | tf_op jit(solution)/shard_map/ppermute | solution.py:16
  162.5 6.1 %collective-permute-start.6 = (bf16[2,2,352]{2,1,0:T(2,128)(2,1)S(1)}, bf16[2,2,352]{2,1,0:T(2,128)(2,1)S(1)}, u32[]{:S(2)}, u32[]{:S(2)}) collective-permute-start(bf16[2,2,352]{2,1,0:T(2,128)(2,1)S(1)} %get-tuple-element.8), channel_id=1, source_target_pairs={{4,0},{8,4},{12,8},{16,12},{20,16},{24,20},{28,24},{5,1},{9,5},{13... | collective-permute-start | bytes 8456 | tf_op jit(solution)/shard_map/ppermute | solution.py:19
  171.9 7.9 %copy-start.1 = (f32[384]{0:T(512)S(1)}, f32[384]{0:T(512)}, u32[]{:S(2)}) copy-start(f32[384]{0:T(512)} %param.14) | copy-start | bytes 4612
Sparse Core Ops, SparseCore 0:
  9.9 42.3 all-gather.2
  54.2 41.7 all-gather.4
  106.7 20.5 reduce-scatter.6
  175.3 22.1 reduce-scatter.8
where the time goes:
time: 216 us; the launch traced here: 215 us
  waiting for transfers between devices  88.5 us (41%)
  blocking collectives  45.4 us (21%)
  matrix products  31.9 us (15%)
  starting transfers between devices  19 us (9%)
  between operations  14.2 us (7%)
  local copies, waits for them, and re-layouts  8.97 us (4%)
  other arithmetic  6.92 us (3%)
    all_gather x1, waiting for transfers between devices, per_device(): lax.all_gather(conv_b, 'seq', axis=1, tiled=True)  35.6 us
    all_gather x1, waiting for transfers between devices, per_device(): lax.all_gather(conv_a, 'seq', axis=1, tiled=True)  27.5 us
    unnamed x6, waiting for transfers between devices  25.4 us
    all_gather x1, blocking collectives, per_device(): act_full = lax.all_gather(act_part, 'ch', axis=2, tiled=True)  16.1 us
    ppermute x4, starting transfers between devices, with_halo(): lax.ppermute(lax.slice_in_dim(block, block.shape[dim] - width, None, axis...  13.7 us
    dot_general x8, matrix products, conv_back(): jnp.einsum('wto,co->wtc', padded[:, start:start + length], weight[offset]...  13.3 us
    dot_general x8, matrix products, conv_rows(): jnp.einsum('wtc,co->wto', padded[:, offset:offset + length], weight[offse...  12.2 us
    psum x1, blocking collectives, per_device(): squares = lax.psum(jnp.sum(mid_f * mid_f, axis=-1, keepdims=True), 'ch')  11.8 us
  transfers between devices with their start and end apart: 12, of which 4 were waited for; matrix products, arithmetic and copies ran while one was open for 16% of the time, Pallas kernels for 0%

commit v1 on v0

--- a/solution.py
+++ b/solution.py
@@ -3,9 +3,16 @@
 import jax.numpy as jnp
 from jax import lax
 from jax.sharding import PartitionSpec as P
+from jax.lax import axis_index, axis_size, ppermute
 
 EPS = 1e-06
 ROOT = math.sqrt(2.0 / math.pi)
+
+
+def build_the_shifts_all(x_local, dim_no):
+    small = list(x_local.shape[1:])
+    small[dim_no] *= x_local.shape[0]
+    return jnp.moveaxis(x_local, 0, dim_no).reshape(small)
 
 
 def with_halo(block, sides, width):
@@ -68,6 +75,24 @@
 
 
 def per_device(dna_features, gain_a, conv_a, bias_a, gain_b, conv_b, bias_b, grad_out):
+
+    def _refer_ports(v0, link_axis, array_dim):
+        n_all = axis_size(link_axis)
+        cards = [(dd, (dd + 1) % n_all) for dd in range(n_all)]
+        n_now, mixed_arr = ([], [])
+        dev_i = 0
+        vals = [(j0, rr) for rr, j0 in cards]
+        while dev_i < n_all - 1:
+            if dev_i % 2 == 0:
+                n_now.append(ppermute(n_now[-1] if n_now else v0, link_axis, cards))
+            else:
+                mixed_arr.append(ppermute(mixed_arr[-1] if mixed_arr else v0, link_axis, vals))
+            dev_i += 1
+        v_next = jnp.stack([*n_now[::-1], v0, *mixed_arr], 0)
+        big = axis_index(link_axis) - len(n_now)
+        v_next = v_next[(jnp.arange(n_all) - big) % n_all]
+        return build_the_shifts_all(v_next, array_dim)
+
     rows_in = dna_features.shape[1]
     rows_mid = rows_in // 2
     width_in = dna_features.shape[2]
@@ -77,7 +102,7 @@
     ch_index = lax.axis_index("ch")
     whole_a, whole_b = (
         lax.all_gather(conv_a, "seq", axis=1, tiled=True),
-        lax.all_gather(conv_b, "seq", axis=1, tiled=True),
+        _refer_ports(conv_b, "seq", 1),
     )
     feat = dna_features.astype(jnp.float32)
     scale_a = lax.rsqrt(jnp.mean(feat * feat, axis=-1, keepdims=True) + EPS)

time: 216 us -> 263 us (1.22)
  local copies, waits for them, and re-layouts: 8.97 us -> 39.8 us
  waiting for transfers between devices: 88.5 us -> 98.4 us
  matrix products: 31.9 us -> 25.4 us
  other arithmetic: 6.92 us -> 11.9 us
  starting transfers between devices: 19 us -> 23.7 us
    ppermute x0 -> x7, waiting for transfers between devices: none -> 45.1 us  [the longest x4 45.1 us: _refer_ports(): n_now.append(ppermute(n_now[-1] if n_now else v0, link_axis, cards))]
    all_gather x1 -> x0, waiting for transfers between devices: 35.6 us -> none  [per_device(): lax.all_gather(conv_b, 'seq', axis=1, tiled=True)]
    unnamed x14 -> x33, local copies, waits for them, and re-layouts: 5.92 us -> 22 us
    unnamed x6 -> x5, waiting for transfers between devices: 25.4 us -> 33.2 us
    all_gather x1, waiting for transfers between devices: 27.5 us -> 20.1 us  [per_device(): lax.all_gather(conv_a, 'seq', axis=1, tiled=True)]
    ppermute x0 -> x7, starting transfers between devices: none -> 6.82 us  [the longest x3 6.27 us: _refer_ports(): ppermute(mixed_arr[-1] if mixed_arr else v0, link_axis, vals)]
    gather x0 -> x1, local copies, waits for them, and re-layouts: none -> 6.28 us  [_refer_ports(): v_next = v_next[(jnp.arange(n_all) - big) % n_all]]
    dot_general x8, matrix products: 13.3 us -> 9.09 us  [conv_back(): jnp.einsum('wto,co->wtc', padded[:, start:start + length], weight[offset]...]
  transfers between devices with their start and end apart: 12 -> 18, of which waited for: 4 -> 7; matrix products, arithmetic and copies ran while one was open for 16% -> 19% of each run, Pallas kernels for 0% -> 0%
where the time goes in v1:
time: 263 us; the launch traced here: 261 us
  waiting for transfers between devices  98.4 us (37%)
  blocking collectives  46.1 us (18%)
  local copies, waits for them, and re-layouts  39.8 us (15%)
  matrix products  25.4 us (10%)
  starting transfers between devices  23.7 us (9%)
  between operations  15.9 us (6%)
  other arithmetic  11.9 us (5%)
    ppermute x4, waiting for transfers between devices, _refer_ports(): n_now.append(ppermute(n_now[-1] if n_now else v0, link_axis, cards))  45.1 us
    unnamed x5, waiting for transfers between devices  33.2 us
    unnamed x33, local copies, waits for them, and re-layouts  22 us
    all_gather x1, waiting for transfers between devices, per_device(): lax.all_gather(conv_a, 'seq', axis=1, tiled=True)  20.1 us
    all_gather x1, blocking collectives, per_device(): act_full = lax.all_gather(act_part, 'ch', axis=2, tiled=True)  17.5 us
    psum x1, blocking collectives, per_device(): squares = lax.psum(jnp.sum(mid_f * mid_f, axis=-1, keepdims=True), 'ch')  11.7 us
    dot_general x8, matrix products, conv_rows(): jnp.einsum('wtc,co->wto', padded[:, offset:offset + length], weight[offse...  11.5 us
    ppermute x4, starting transfers between devices, with_halo(): lax.ppermute(lax.slice_in_dim(block, block.shape[dim] - width, None, axis...  11.4 us
  transfers between devices with their start and end apart: 18, of which 7 were waited for; matrix products, arithmetic and copies ran while one was open for 19% of the time, Pallas kernels for 0%

profile of v1, /device:TPU:0, one launch (start us, length us, event | category | flops | bytes accessed | tf_op | source)
XLA Modules:
  0.0 261.2 jit_solution(12876275843156620395)
XLA Ops:
  8.6 11.6 %collective-permute-done.3 = bf16[5,176,384]{2,1,0:T(8,128)(2,1)S(1)} collective-permute-done((bf16[5,176,384]{2,1,0:T(8,128)(2,1)}, bf16[5,176,384]{2,1,0:T(8,128)(2,1)S(1)}, u32[]{:S(2)}, u32[]{:S(2)}) %collective-permute-start.3) | collective-permute-done | bytes 675872 | tf_op jit(solution)/shard_map/ppermute | solution.py:87
  20.2 2.6 %collective-permute-start.7 = (bf16[5,176,384]{2,1,0:T(8,128)(2,1)}, bf16[5,176,384]{2,1,0:T(8,128)(2,1)S(1)}, u32[]{:S(2)}, u32[]{:S(2)}) collective-permute-start(bf16[5,176,384]{2,1,0:T(8,128)(2,1)} %param.13), channel_id=1, source_target_pairs={{4,0},{8,4},{12,8},{16,12},{20,16},{24,20},{28,24},{0,28},{5,1},{9... | collective-permute-start | bytes 2027528 | tf_op jit(solution)/shard_map/ppermute | solution.py:89
  22.8 13.8 %collective-permute-done.4 = bf16[5,176,384]{2,1,0:T(8,128)(2,1)S(1)} collective-permute-done((bf16[5,176,384]{2,1,0:T(8,128)(2,1)S(1)}, bf16[5,176,384]{2,1,0:T(8,128)(2,1)S(1)}, u32[]{:S(2)}, u32[]{:S(2)}) %collective-permute-start.4) | collective-permute-done | bytes 675872 | tf_op jit(solution)/shard_map/ppermute | solution.py:87
  36.6 2.7 %collective-permute-start.8 = (bf16[5,176,384]{2,1,0:T(8,128)(2,1)S(1)}, bf16[5,176,384]{2,1,0:T(8,128)(2,1)}, u32[]{:S(2)}, u32[]{:S(2)}) collective-permute-start(bf16[5,176,384]{2,1,0:T(8,128)(2,1)S(1)} %collective-permute-done.7), channel_id=1, source_target_pairs={{4,0},{8,4},{12,8},{16,12},{20,16},{24,20},{28,24},{0,28},{5,1},{9... | collective-permute-start | bytes 2027528 | tf_op jit(solution)/shard_map/ppermute | solution.py:89
  39.3 14.5 %collective-permute-done.5 = bf16[5,176,384]{2,1,0:T(8,128)(2,1)} collective-permute-done((bf16[5,176,384]{2,1,0:T(8,128)(2,1)S(1)}, bf16[5,176,384]{2,1,0:T(8,128)(2,1)}, u32[]{:S(2)}, u32[]{:S(2)}) %collective-permute-start.5) | collective-permute-done | bytes 675872 | tf_op jit(solution)/shard_map/ppermute | solution.py:87
  54.6 1.3 collective-permute-start.11
  55.9 3.0 %collective-permute-start.12 = (bf16[2,2,384]{2,1,0:T(2,128)(2,1)S(1)}, bf16[2,2,384]{2,1,0:T(2,128)(2,1)S(1)}, u32[]{:S(2)}, u32[]{:S(2)}) collective-permute-start(bf16[2,2,384]{2,1,0:T(2,128)(2,1)S(1)} %get-tuple-element.18), channel_id=1, source_target_pairs={{0,4},{4,8},{8,12},{12,16},{16,20},{20,24},{24,28},{1,5},{5,9},{9,... | collective-permute-start | bytes 9224 | tf_op jit(solution)/shard_map/ppermute | solution.py:23
  59.1 1.0 collective-permute-start.9
  60.0 5.2 %collective-permute-done.6 = bf16[5,176,384]{2,1,0:T(8,128)(2,1)} collective-permute-done((bf16[5,176,384]{2,1,0:T(8,128)(2,1)}, bf16[5,176,384]{2,1,0:T(8,128)(2,1)}, u32[]{:S(2)}, u32[]{:S(2)}) %collective-permute-start.6) | collective-permute-done | bytes 675872 | tf_op jit(solution)/shard_map/ppermute | solution.py:87
  65.2 2.0 bitcast_dynamic-update-slice_fusion.7
  67.2 2.0 bitcast_dynamic-update-slice_fusion.6
  69.3 0.9 bitcast_dynamic-update-slice_fusion.5
  70.2 0.9 bitcast_dynamic-update-slice_fusion.4
  71.1 0.9 bitcast_dynamic-update-slice_fusion.3
  72.0 0.9 bitcast_dynamic-update-slice_fusion.2
  73.0 2.0 bitcast_dynamic-update-slice_fusion.1
  75.0 0.9 bitcast_dynamic-update-slice_fusion
  75.9 6.3 %gather_fusion = bf16[8,5,176,384]{3,2,1,0:T(8,128)(2,1)} fusion(bf16[8,5,176,384]{3,2,1,0:T(8,128)(2,1)} %bitcast_dynamic-update-slice_fusion, s32[1024]{0:T(1024)S(1)} %pad_clamp_fusion), kind=kCustom, calls=%fused_computation | custom fusion | bytes 10813472 | tf_op jit(solution)/shard_map/gather | solution.py:93
  82.2 3.1 %fusion.90 = (bf16[1,8,176,384]{3,2,0,1:T(8,128)(2,1)S(1)}, bf16[1,8,176,384]{3,2,0,1:T(8,128)(2,1)S(1)}, bf16[1,8,176,384]{3,2,0,1:T(8,128)(2,1)S(1)}, bf16[1,8...) fusion(bf16[5,8,176,384]{3,2,0,1:T(8,128)(2,1)} %bitcast.96), kind=kLoop, calls=%fused_computation.152 | loop fusion | bytes 10813440 | tf_op jit(solution)/shard_map/slice | solution.py:56
  88.2 1.8 copy.34
  90.0 2.7 %reshape.113 = bf16[1408,64]{1,0:T(8,128)(2,1)} reshape(bf16[1408,2,32]{2,1,0:T(2,128)(2,1)} %bitcast.107) | data formatting | bytes 360448
  93.3 1.1 multiply_reduce_fusion
  94.4 1.3 fusion.22
  96.5 2.3 collective-permute-start
  98.8 1.3 collective-permute-start.1
  100.1 1.9 convert_element_type.60
  102.1 0.8 dynamic_slice.9
  102.9 15.7 %reduce-scatter.7.cloned.1.call-done = bf16[352,64]{1,0:T(8,128)(2,1)} async-done(((bf16[1408,64]{1,0:T(8,128)(2,1)}), bf16[352,64]{1,0:T(8,128)(2,1)}) %reduce-scatter.7.cloned.1.call-update) | async-done | bytes 45072
  118.5 1.0 reshape.114
  119.7 20.1 %all-gather.2.cloned.1.call-done = bf16[5,1280,352]{2,1,0:T(8,128)(2,1)} async-done(((bf16[5,160,352]{2,1,0:T(8,128)(2,1)}), bf16[5,1280,352]{2,1,0:T(8,128)(2,1)}) %all-gather.2.cloned.1.call-update) | async-done | bytes 4505616 | tf_op jit(solution)/shard_map/all_gather | solution.py:104
  139.8 1.7 fusion.15
  141.5 1.6 fusion.13
  143.2 1.6 fusion.17
  144.8 1.5 fusion.8
  146.4 2.2 fusion.7
  148.6 1.0 reshape.93
  149.6 0.9 reduce_sum.55
  150.5 1.0 fusion.62
  151.5 11.7 %psum.21 = f32[2,32,1]{1,0,2:T(2,128)S(1)} all-reduce(f32[2,32,1]{1,0,2:T(2,128)S(1)} %bitcast.111), channel_id=1, replica_groups=mesh['seq'=8,'ch'=4] {'ch'}, use_global_device_ids=true, to_apply=%region_3.4 | all-reduce | flops 64 | bytes 512 | tf_op jit(solution)/shard_map/psum | solution.py:115
  163.4 8.4 %psum.22 = f32[2,32,1]{1,0,2:T(2,128)S(1)} all-reduce(f32[2,32,1]{1,0,2:T(2,128)S(1)} %bitcast.112), channel_id=1, replica_groups=mesh['seq'=8,'ch'=4] {'ch'}, use_global_device_ids=true, to_apply=%region_7.8 | all-reduce | flops 64 | bytes 512 | tf_op jit(solution)/shard_map/psum | solution.py:130
  171.8 0.8 multiply_convert_fusion.1
  172.8 17.5 %all_gather.7 = bf16[2,32,1408]{1,0,2:T(2,128)(2,1)} all-gather(bf16[2,32,352]{1,0,2:T(2,128)(2,1)S(1)} %copy.28), channel_id=1, replica_groups=mesh['seq'=8,'ch'=4] {'ch'}, dimensions={2}, use_global_device_ids=true | all-gather | bytes 225280 | tf_op jit(solution)/shard_map/all_gather | solution.py:118
  190.3 2.2 copy.29
  193.1 2.2 fusion.95
  195.3 1.5 broadcast_in_dim.13
  196.7 1.0 convert_element_type.74
  197.7 1.3 collective-permute-start.13
  199.0 3.0 %collective-permute-start.14 = (bf16[2,2,352]{2,1,0:T(2,128)(2,1)S(1)}, bf16[2,2,352]{2,1,0:T(2,128)(2,1)S(1)}, u32[]{:S(2)}, u32[]{:S(2)}) collective-permute-start(bf16[2,2,352]{2,1,0:T(2,128)(2,1)S(1)} %get-tuple-element.14), channel_id=1, source_target_pairs={{0,4},{4,8},{8,12},{12,16},{16,20},{20,24},{24,28},{1,5},{5,9},{9,... | collective-permute-start | bytes 8456 | tf_op jit(solution)/shard_map/ppermute | solution.py:23
  202.1 3.0 %collective-permute-start.2 = (bf16[2,2,1408]{2,1,0:T(2,128)(2,1)}, bf16[2,2,1408]{2,1,0:T(2,128)(2,1)S(1)}, u32[]{:S(2)}, u32[]{:S(2)}) collective-permute-start(bf16[2,2,1408]{2,1,0:T(2,128)(2,1)} %get-tuple-element.11), channel_id=1, source_target_pairs={{0,4},{4,8},{8,12},{12,16},{16,20},{20,24},{24,28},{1,5},{5,9},{9,... | collective-permute-start | bytes 33800 | tf_op jit(solution)/shard_map/ppermute | solution.py:23
  205.1 1.5 collective-permute-start.10
  206.6 1.6 fusion.14
  208.3 1.6 fusion.12
  209.9 1.6 fusion.16
  211.5 1.6 fusion.1
  213.1 2.4 fusion.2
  215.5 2.1 copy.36
  217.6 2.2 reshape.115
  219.8 1.5 fusion.42
  221.3 1.2 fusion.11
  224.0 16.9 %reduce-scatter.9.cloned.1.call-done = bf16[320,128]{1,0:T(8,128)(2,1)} async-done(((bf16[1280,128]{1,0:T(8,128)(2,1)}), bf16[320,128]{1,0:T(8,128)(2,1)}) %reduce-scatter.9.cloned.1.call-update) | async-done | bytes 81936
  240.9 1.0 reshape.116
  242.1 1.3 multiply_reduce_fusion.1
  243.3 8.5 %psum.23 = f32[2,64,1]{1,0,2:T(2,128)S(1)} all-reduce(f32[2,64,1]{1,0,2:T(2,128)S(1)} %bitcast.113), channel_id=1, replica_groups=mesh['seq'=8,'ch'=4] {'ch'}, use_global_device_ids=true, to_apply=%region_10.11 | all-reduce | flops 128 | bytes 1024 | tf_op jit(solution)/shard_map/psum | solution.py:142
  251.9 1.8 multiply_convert_fusion
  (69 shorter events, 8.5 us)
Async XLA Ops:
  8.0 63.1 %copy-start.2 = (bf16[5,176,384]{2,1,0:T(8,128)(2,1)S(1)}, bf16[5,176,384]{2,1,0:T(8,128)(2,1)}, u32[]{:S(2)}) copy-start(bf16[5,176,384]{2,1,0:T(8,128)(2,1)} %param.13) | copy-start | bytes 2027524
  8.0 110.5 %reduce-scatter.7.cloned.1.call-start = ((), (), s32[]{:S(2)}) async-start(), calls=%async_computation.3 | async-start | bytes 450560
  8.1 12.1 %collective-permute-start.3 = (bf16[5,176,384]{2,1,0:T(8,128)(2,1)}, bf16[5,176,384]{2,1,0:T(8,128)(2,1)S(1)}, u32[]{:S(2)}, u32[]{:S(2)}) collective-permute-start(bf16[5,176,384]{2,1,0:T(8,128)(2,1)} %param.13), channel_id=1, source_target_pairs={{0,4},{4,8},{8,12},{12,16},{16,20},{20,24},{24,28},{28,0},{1,5},{5... | collective-permute-start | bytes 2027528 | tf_op jit(solution)/shard_map/ppermute | solution.py:87
  20.2 16.5 %collective-permute-start.4 = (bf16[5,176,384]{2,1,0:T(8,128)(2,1)S(1)}, bf16[5,176,384]{2,1,0:T(8,128)(2,1)S(1)}, u32[]{:S(2)}, u32[]{:S(2)}) collective-permute-start(bf16[5,176,384]{2,1,0:T(8,128)(2,1)S(1)} %collective-permute-done.3), channel_id=1, source_target_pairs={{0,4},{4,8},{8,12},{12,16},{16,20},{20,24},{24,28},{28,0},{1,5},{5... | collective-permute-start | bytes 2027528 | tf_op jit(solution)/shard_map/ppermute | solution.py:87
  20.2 16.5 %collective-permute-start.7 = (bf16[5,176,384]{2,1,0:T(8,128)(2,1)}, bf16[5,176,384]{2,1,0:T(8,128)(2,1)S(1)}, u32[]{:S(2)}, u32[]{:S(2)}) collective-permute-start(bf16[5,176,384]{2,1,0:T(8,128)(2,1)} %param.13), channel_id=1, source_target_pairs={{4,0},{8,4},{12,8},{16,12},{20,16},{24,20},{28,24},{0,28},{5,1},{9... | collective-permute-start | bytes 2027528 | tf_op jit(solution)/shard_map/ppermute | solution.py:89
  36.6 17.2 %collective-permute-start.5 = (bf16[5,176,384]{2,1,0:T(8,128)(2,1)S(1)}, bf16[5,176,384]{2,1,0:T(8,128)(2,1)}, u32[]{:S(2)}, u32[]{:S(2)}) collective-permute-start(bf16[5,176,384]{2,1,0:T(8,128)(2,1)S(1)} %collective-permute-done.4), channel_id=1, source_target_pairs={{0,4},{4,8},{8,12},{12,16},{16,20},{20,24},{24,28},{28,0},{1,5},{5... | collective-permute-start | bytes 2027528 | tf_op jit(solution)/shard_map/ppermute | solution.py:87
  36.6 22.4 %collective-permute-start.8 = (bf16[5,176,384]{2,1,0:T(8,128)(2,1)S(1)}, bf16[5,176,384]{2,1,0:T(8,128)(2,1)}, u32[]{:S(2)}, u32[]{:S(2)}) collective-permute-start(bf16[5,176,384]{2,1,0:T(8,128)(2,1)S(1)} %collective-permute-done.7), channel_id=1, source_target_pairs={{4,0},{8,4},{12,8},{16,12},{20,16},{24,20},{28,24},{0,28},{5,1},{9... | collective-permute-start | bytes 2027528 | tf_op jit(solution)/shard_map/ppermute | solution.py:89
  53.8 11.4 %collective-permute-start.6 = (bf16[5,176,384]{2,1,0:T(8,128)(2,1)}, bf16[5,176,384]{2,1,0:T(8,128)(2,1)}, u32[]{:S(2)}, u32[]{:S(2)}) collective-permute-start(bf16[5,176,384]{2,1,0:T(8,128)(2,1)} %collective-permute-done.5), channel_id=1, source_target_pairs={{0,4},{4,8},{8,12},{12,16},{16,20},{20,24},{24,28},{28,0},{1,5},{5... | collective-permute-start | bytes 2027528 | tf_op jit(solution)/shard_map/ppermute | solution.py:87
  54.6 4.4 %collective-permute-start.11 = (bf16[2,2,384]{2,1,0:T(2,128)(2,1)S(1)}, bf16[2,2,384]{2,1,0:T(2,128)(2,1)S(1)}, u32[]{:S(2)}, u32[]{:S(2)}) collective-permute-start(bf16[2,2,384]{2,1,0:T(2,128)(2,1)S(1)} %get-tuple-element.17), channel_id=1, source_target_pairs={{4,0},{8,4},{12,8},{16,12},{20,16},{24,20},{28,24},{5,1},{9,5},{13... | collective-permute-start | bytes 9224 | tf_op jit(solution)/shard_map/ppermute | solution.py:26
  55.9 31.3 %collective-permute-start.12 = (bf16[2,2,384]{2,1,0:T(2,128)(2,1)S(1)}, bf16[2,2,384]{2,1,0:T(2,128)(2,1)S(1)}, u32[]{:S(2)}, u32[]{:S(2)}) collective-permute-start(bf16[2,2,384]{2,1,0:T(2,128)(2,1)S(1)} %get-tuple-element.18), channel_id=1, source_target_pairs={{0,4},{4,8},{8,12},{12,16},{16,20},{20,24},{24,28},{1,5},{5,9},{9,... | collective-permute-start | bytes 9224 | tf_op jit(solution)/shard_map/ppermute | solution.py:23
  59.1 15.9 %collective-permute-start.9 = (bf16[5,176,384]{2,1,0:T(8,128)(2,1)}, bf16[5,176,384]{2,1,0:T(8,128)(2,1)S(1)}, u32[]{:S(2)}, u32[]{:S(2)}) collective-permute-start(bf16[5,176,384]{2,1,0:T(8,128)(2,1)} %collective-permute-done.8), channel_id=1, source_target_pairs={{4,0},{8,4},{12,8},{16,12},{20,16},{24,20},{28,24},{0,28},{5,1},{9... | collective-permute-start | bytes 2027528 | tf_op jit(solution)/shard_map/ppermute | solution.py:89
  85.3 1.0 copy-start
  85.3 1.5 copy-start.1
  86.3 8.1 %copy-start.5 = (f32[1280]{0:T(1024)S(1)}, f32[1280]{0:T(1024)}, u32[]{:S(2)}) copy-start(f32[1280]{0:T(1024)} %param.9) | copy-start | bytes 15364
  92.7 47.1 %all-gather.2.cloned.1.call-start = ((), (), s32[]{:S(2)}) async-start(), calls=%async_computation.2 | async-start | bytes 5529600 | tf_op jit(solution)/shard_map/all_gather | solution.py:104
  93.3 147.7 %reduce-scatter.9.cloned.1.call-start = ((), (), s32[]{:S(2)}) async-start(), calls=%async_computation.4 | async-start | bytes 409600
  94.4 51.9 %copy-start.7 = (f32[352]{0:T(512)S(1)}, f32[352]{0:T(512)}, u32[]{:S(2)}) copy-start(f32[352]{0:T(512)} %param.11) | copy-start | bytes 4228
  95.8 0.7 copy-start.3
  96.5 45.0 %collective-permute-start = (bf16[2,2,1280]{2,1,0:T(2,128)(2,1)S(1)}, bf16[2,2,1280]{2,1,0:T(2,128)(2,1)S(1)}, u32[]{:S(2)}, u32[]{:S(2)}) collective-permute-start(bf16[2,2,1280]{2,1,0:T(2,128)(2,1)S(1)} %get-tuple-element.9), channel_id=1, source_target_pairs={{0,4},{4,8},{8,12},{12,16},{16,20},{20,24},{24,28},{1,5},{5,9},{9,... | collective-permute-start | bytes 30728 | tf_op jit(solution)/shard_map/ppermute | solution.py:23
  98.8 44.4 %collective-permute-start.1 = (bf16[2,2,1280]{2,1,0:T(2,128)(2,1)S(1)}, bf16[2,2,1280]{2,1,0:T(2,128)(2,1)S(1)}, u32[]{:S(2)}, u32[]{:S(2)}) collective-permute-start(bf16[2,2,1280]{2,1,0:T(2,128)(2,1)S(1)} %get-tuple-element.10), channel_id=1, source_target_pairs={{4,0},{8,4},{12,8},{16,12},{20,16},{24,20},{28,24},{5,1},{9,5},{13... | collective-permute-start | bytes 30728 | tf_op jit(solution)/shard_map/ppermute | solution.py:26
  139.8 5.0 %copy-start.4 = (bf16[2,64,1280]{2,1,0:T(8,128)(2,1)S(1)}, bf16[2,64,1280]{2,1,0:T(8,128)(2,1)}, u32[]{:S(2)}) copy-start(bf16[2,64,1280]{2,1,0:T(8,128)(2,1)} %copy-done.3) | copy-start | bytes 983044
  197.7 10.5 %collective-permute-start.13 = (bf16[2,2,352]{2,1,0:T(2,128)(2,1)S(1)}, bf16[2,2,352]{2,1,0:T(2,128)(2,1)S(1)}, u32[]{:S(2)}, u32[]{:S(2)}) collective-permute-start(bf16[2,2,352]{2,1,0:T(2,128)(2,1)S(1)} %get-tuple-element.13), channel_id=1, source_target_pairs={{4,0},{8,4},{12,8},{16,12},{20,16},{24,20},{28,24},{5,1},{9,5},{13... | collective-permute-start | bytes 8456 | tf_op jit(solution)/shard_map/ppermute | solution.py:26
  199.0 10.8 %collective-permute-start.14 = (bf16[2,2,352]{2,1,0:T(2,128)(2,1)S(1)}, bf16[2,2,352]{2,1,0:T(2,128)(2,1)S(1)}, u32[]{:S(2)}, u32[]{:S(2)}) collective-permute-start(bf16[2,2,352]{2,1,0:T(2,128)(2,1)S(1)} %get-tuple-element.14), channel_id=1, source_target_pairs={{0,4},{4,8},{8,12},{12,16},{16,20},{20,24},{24,28},{1,5},{5,9},{9,... | collective-permute-start | bytes 8456 | tf_op jit(solution)/shard_map/ppermute | solution.py:23
  202.1 17.7 %collective-permute-start.2 = (bf16[2,2,1408]{2,1,0:T(2,128)(2,1)}, bf16[2,2,1408]{2,1,0:T(2,128)(2,1)S(1)}, u32[]{:S(2)}, u32[]{:S(2)}) collective-permute-start(bf16[2,2,1408]{2,1,0:T(2,128)(2,1)} %get-tuple-element.11), channel_id=1, source_target_pairs={{0,4},{4,8},{8,12},{12,16},{16,20},{20,24},{24,28},{1,5},{5,9},{9,... | collective-permute-start | bytes 33800 | tf_op jit(solution)/shard_map/ppermute | solution.py:23
  205.1 17.4 %collective-permute-start.10 = (bf16[2,2,1408]{2,1,0:T(2,128)(2,1)}, bf16[2,2,1408]{2,1,0:T(2,128)(2,1)S(1)}, u32[]{:S(2)}, u32[]{:S(2)}) collective-permute-start(bf16[2,2,1408]{2,1,0:T(2,128)(2,1)} %get-tuple-element.12), channel_id=1, source_target_pairs={{4,0},{8,4},{12,8},{16,12},{20,16},{24,20},{28,24},{5,1},{9,5},{13... | collective-permute-start | bytes 33800 | tf_op jit(solution)/shard_map/ppermute | solution.py:26
  215.5 7.3 %copy-start.6 = (f32[384]{0:T(512)S(1)}, f32[384]{0:T(512)}, u32[]{:S(2)}) copy-start(f32[384]{0:T(512)} %param.14) | copy-start | bytes 4612
Sparse Core Ops, SparseCore 0:
  92.8 25.6 reduce-scatter.6
  219.9 20.9 reduce-scatter.8
Sparse Core Ops, SparseCore 1:
  95.1 44.7 all-gather.1
